TPU v7x, 32 devices: a whole 2x2x4 slice. The times are simulated.
32 devices in a mesh: ctx: 16 (over z, y, core), head: 2 (over x).
Axes of the slice: x: 2, y: 2, z: 4, core: 2. Of those that a mesh axis runs over, the one named last changes fastest.
Arguments:
- loader_query_rows: bfloat16 [6144, 8192], P(('ctx', 'head')), may hold values from -6 to 6
- loader_key_rows: bfloat16 [6144, 1024], P(('ctx', 'head')), may hold values from -6 to 6
- loader_value_rows: bfloat16 [6144, 1024], P(('ctx', 'head')), may hold values from -6 to 6
- output_gradient_rows: bfloat16 [6144, 8192], P(('ctx', 'head')), may hold values from -6 to 6
- doc_blocks: int32 [2, 3], replicated, may hold values from 1 to 16, as said below
- block_perm: int32 [48], replicated, may hold values from 0 to 47, as said below
Outputs:
- attn_out: bfloat16 [6144, 8192], P('ctx', 'head')
- grad_query: bfloat16 [6144, 8192], P('ctx', 'head')
- key_gradient: bfloat16 [6144, 1024], P('ctx', 'head')
- value_gradient: bfloat16 [6144, 1024], P('ctx', 'head')
Inputs may be any that keep to these rules, and one draw needn't show every extreme that they name: doc_blocks[g] lists in order the lengths, in blocks, of the documents that fill row blocks g * 24 to (g + 1) * 24 - 1 of the packed row; each row sums to 24 and holds one length equal to 16. block_perm is a permutation that maps the blocks of each aligned span of 24 blocks onto the same span.
All inputs are finite; a program needn't handle non-finite values.
Results may differ from a plain program's by a relative error of at most 0.012.
The roundings to bfloat16 on the way count: a program that leaves them out, or rounds other values in their place, can miss the bound.
Values may be sent and summed in bfloat16 or wider, within the bound.
A program may use at most 192 MiB of HBM per device.

v0:
```python
from functools import partial

import jax
import jax.numpy as jnp
from jax import lax
from jax.sharding import PartitionSpec as P

QUERY_HEADS = 64
KEY_VALUE_HEADS = 8
HEAD_SIZE = 128
MASK_BLOCK_SIZE = 128
GROUP_DEV = 8
GROUP_BLOCKS = 24
MOST = 16


MASKED_LOGIT = -1e30


def from_partner(value, axis, stride):
    mask = 2**stride
    pairs = [(source, source ^ mask) for source in range(lax.axis_size(axis))]
    return lax.ppermute(value, axis, pairs)


def doc_first(doc_blocks, total_blocks):
    doc_ends = jnp.cumsum(doc_blocks, axis=1)
    span_base = jnp.arange(doc_blocks.shape[0], dtype=jnp.int32)[:, None] * GROUP_BLOCKS
    firsts = (span_base + doc_ends - doc_blocks).reshape(-1)
    blocks = jnp.arange(total_blocks, dtype=jnp.int32)
    return jnp.max(jnp.where(firsts[None, :] <= blocks[:, None], firsts[None, :], 0), axis=1)


def inverse_of(block_perm):
    places = jnp.arange(block_perm.shape[0], dtype=jnp.int32)
    matches = block_perm[None, :] == places[:, None]
    return jnp.sum(jnp.where(matches, places[None, :], 0), axis=1)


def row_block_of(loader_block):
    span_start = loader_block // GROUP_BLOCKS * GROUP_BLOCKS
    return span_start + (loader_block - span_start + GROUP_BLOCKS // 2) % GROUP_BLOCKS


def bit_order(depth_levels):
    return list(range(depth_levels - 1, -1, -1))


def upper_bit(own_index, bit_index):
    return own_index // (1 << bit_index) % 2 == 1


def scores(query_block, key_block, on_diagonal):
    raw_logits = jnp.einsum(
        "tgrd,kgd->tgrk", query_block, key_block, preferred_element_type=jnp.float32
    ) * HEAD_SIZE ** (-0.5)
    above_diagonal = lax.broadcasted_iota(
        jnp.int32, (MASK_BLOCK_SIZE, 1, 1, MASK_BLOCK_SIZE), 3
    ) > lax.broadcasted_iota(jnp.int32, (MASK_BLOCK_SIZE, 1, 1, MASK_BLOCK_SIZE), 0)
    return jnp.where(above_diagonal & on_diagonal, MASKED_LOGIT, raw_logits)


def move_blocks(first_rows, second_rows, inverse):
    per_device = first_rows.shape[0] // MASK_BLOCK_SIZE
    row_width = first_rows.shape[1]
    spread = (
        lax.all_to_all(
            first_rows.reshape(per_device, MASK_BLOCK_SIZE, row_width),
            "ctx",
            split_axis=1,
            concat_axis=0,
            tiled=True,
        ),
        lax.all_to_all(
            second_rows.reshape(per_device, MASK_BLOCK_SIZE, row_width),
            "ctx",
            split_axis=1,
            concat_axis=0,
            tiled=True,
        ),
    )
    moved_rows = (
        lax.all_to_all(spread[0][inverse], "ctx", split_axis=0, concat_axis=1, tiled=True),
        lax.all_to_all(spread[1][inverse], "ctx", split_axis=0, concat_axis=1, tiled=True),
    )
    return (moved_rows[0].reshape(-1, row_width), moved_rows[1].reshape(-1, row_width))


def kv_block(kv_group, block_id, group_first):
    row_local = block_id - group_first
    local_block = (row_local + GROUP_BLOCKS - GROUP_BLOCKS // 2) % GROUP_BLOCKS
    per_device = kv_group.shape[2] // MASK_BLOCK_SIZE
    width_kv = kv_group.shape[3]
    kv_piece = lax.dynamic_slice(
        kv_group,
        (local_block // per_device, 0, local_block % per_device * MASK_BLOCK_SIZE, 0),
        (1, 2, MASK_BLOCK_SIZE, width_kv),
    )
    kv_heads = width_kv // HEAD_SIZE
    return (
        kv_piece[0, 0].reshape(MASK_BLOCK_SIZE, kv_heads, HEAD_SIZE),
        kv_piece[0, 1].reshape(MASK_BLOCK_SIZE, kv_heads, HEAD_SIZE),
    )


def attend_block(kv_group, firsts, group_first, running_totals, scan_item):
    query_block, grad_block, block_id = scan_item
    logit_scale = HEAD_SIZE ** (-0.5)
    doc_start = firsts[block_id]
    key_count = block_id - doc_start + 1
    row_shape = query_block.shape[:3]

    def fetch_block(step_index):
        current = doc_start + step_index
        key_block, value_block = kv_block(kv_group, current, group_first)
        return (current, key_block, value_block)

    def softmax_stats(step_index, loop_state):
        row_max, row_sum, logit_store = loop_state
        current, key_block, value_block = fetch_block(step_index)
        logits = scores(query_block, key_block, current == block_id)
        logit_store = lax.dynamic_update_index_in_dim(logit_store, logits, step_index, 0)
        new_max = jnp.maximum(row_max, jnp.max(logits, axis=3))
        row_sum = row_sum * jnp.exp(row_max - new_max) + jnp.sum(
            jnp.exp(logits - new_max[..., None]), axis=3
        )
        return (new_max, row_sum, logit_store)

    empty_store = jnp.zeros((MOST,) + row_shape + (MASK_BLOCK_SIZE,), jnp.float32)
    row_max, row_sum, logit_store = lax.fori_loop(
        0,
        key_count,
        softmax_stats,
        (
            jnp.full(row_shape, MASKED_LOGIT, jnp.float32),
            jnp.zeros(row_shape, jnp.float32),
            empty_store,
        ),
    )
    log_total = row_max + jnp.log(row_sum)

    def mix_values(step_index, out_total):
        current, key_block, value_block = fetch_block(step_index)
        logits = lax.dynamic_index_in_dim(logit_store, step_index, 0, keepdims=False)
        weights_low = jnp.exp(logits - log_total[..., None]).astype(jnp.bfloat16)
        return out_total + jnp.einsum(
            "tgrk,kgd->tgrd", weights_low, value_block, preferred_element_type=jnp.float32
        )

    output = lax.fori_loop(
        0, key_count, mix_values, jnp.zeros(query_block.shape, jnp.float32)
    ).astype(jnp.bfloat16)
    delta_rows = jnp.sum(grad_block.astype(jnp.float32) * output.astype(jnp.float32), axis=-1)

    def backprop(step_index, loop_state):
        grad_total, running_totals = loop_state
        current, key_block, value_block = fetch_block(step_index)
        logits = lax.dynamic_index_in_dim(logit_store, step_index, 0, keepdims=False)
        weights = jnp.exp(logits - log_total[..., None])
        weights_low = weights.astype(jnp.bfloat16)
        value_part = jnp.einsum(
            "tgrk,tgrd->kgd", weights_low, grad_block, preferred_element_type=jnp.float32
        )
        grad_weights = jnp.einsum(
            "tgrd,kgd->tgrk", grad_block, value_block, preferred_element_type=jnp.float32
        )
        dlogits = (weights * (grad_weights - delta_rows[..., None])).astype(jnp.bfloat16)
        grad_total = grad_total + jnp.einsum(
            "tgrk,kgd->tgrd", dlogits, key_block, preferred_element_type=jnp.float32
        )
        key_part = (
            jnp.einsum("tgrk,tgrd->kgd", dlogits, query_block, preferred_element_type=jnp.float32)
            * logit_scale
        )
        grad_part = jnp.stack([key_part, value_part]).reshape(
            2, 1, MASK_BLOCK_SIZE, running_totals.shape[3]
        )
        local_block = current - group_first
        previous = lax.dynamic_slice(running_totals, (0, local_block, 0, 0), grad_part.shape)
        running_totals = lax.dynamic_update_slice(
            running_totals, previous + grad_part, (0, local_block, 0, 0)
        )
        return (grad_total, running_totals)

    grad_total, running_totals = lax.fori_loop(
        0, key_count, backprop, (jnp.zeros(query_block.shape, jnp.float32), running_totals)
    )
    return (running_totals, (output, (grad_total * logit_scale).astype(jnp.bfloat16)))


def body(
    loader_query_rows,
    loader_key_rows,
    loader_value_rows,
    output_gradient_rows,
    doc_blocks,
    block_perm,
):
    loader_query_rows, loader_key_rows, loader_value_rows, output_gradient_rows = (
        lax.all_to_all(loader_query_rows, "head", split_axis=1, concat_axis=0, tiled=True),
        lax.all_to_all(loader_key_rows, "head", split_axis=1, concat_axis=0, tiled=True),
        lax.all_to_all(loader_value_rows, "head", split_axis=1, concat_axis=0, tiled=True),
        lax.all_to_all(output_gradient_rows, "head", split_axis=1, concat_axis=0, tiled=True),
    )
    tokens = loader_query_rows.shape[0]
    per_device = tokens // MASK_BLOCK_SIZE
    width_kv = loader_key_rows.shape[1]
    width_query = loader_query_rows.shape[1]
    kv_heads = width_kv // HEAD_SIZE
    query_group_ratio = QUERY_HEADS // KEY_VALUE_HEADS
    own_index = lax.axis_index("ctx")
    depth_levels = GROUP_DEV.bit_length() - 1
    firsts = doc_first(doc_blocks, block_perm.shape[0])
    inverse = inverse_of(block_perm)
    group_first = own_index // GROUP_DEV * GROUP_BLOCKS
    own_blocks = own_index * per_device + jnp.arange(per_device, dtype=jnp.int32)
    collected = jnp.stack([loader_key_rows, loader_value_rows]).reshape(
        (1,) * depth_levels + (2, tokens, width_kv)
    )
    for bit_index in bit_order(depth_levels):
        axis_pos = depth_levels - 1 - bit_index
        partner = from_partner(collected, "ctx", bit_index)
        collected = jnp.where(
            upper_bit(own_index, bit_index),
            jnp.concatenate([partner, collected], axis_pos),
            jnp.concatenate([collected, partner], axis_pos),
        )
    kv_group = collected.reshape(GROUP_DEV, 2, tokens, width_kv)
    loader_query_rows, output_gradient_rows = move_blocks(
        loader_query_rows, output_gradient_rows, inverse
    )
    query_ids = row_block_of(inverse[own_blocks])
    query_blocks = loader_query_rows.reshape(
        per_device, MASK_BLOCK_SIZE, kv_heads, query_group_ratio, HEAD_SIZE
    )
    grad_blocks = output_gradient_rows.reshape(
        per_device, MASK_BLOCK_SIZE, kv_heads, query_group_ratio, HEAD_SIZE
    )
    empty_totals = jnp.zeros((2, GROUP_BLOCKS, MASK_BLOCK_SIZE, width_kv), jnp.float32)
    running_totals, (attn_blocks, query_grad_blocks) = lax.scan(
        partial(attend_block, kv_group, firsts, group_first),
        empty_totals,
        (query_blocks, grad_blocks, query_ids),
    )
    attn_rows = attn_blocks.reshape(tokens, width_query)
    query_grad_rows = query_grad_blocks.reshape(tokens, width_query)
    loader_local = lax.dynamic_slice_in_dim(inverse, group_first, GROUP_BLOCKS) - group_first
    local_order = (loader_local + GROUP_BLOCKS // 2) % GROUP_BLOCKS
    shaped = running_totals[:, local_order].reshape(
        (2,) + (2,) * depth_levels + (per_device, MASK_BLOCK_SIZE, width_kv)
    )
    for bit_index in bit_order(depth_levels):
        axis_pos = 1 + depth_levels - 1 - bit_index
        lower_half = lax.slice_in_dim(shaped, 0, 1, axis=axis_pos)
        upper_slice = lax.slice_in_dim(shaped, 1, 2, axis=axis_pos)
        upper_half = upper_bit(own_index, bit_index)
        kept_half = jnp.where(upper_half, upper_slice, lower_half)
        sent_half = jnp.where(upper_half, lower_half, upper_slice)
        shaped = kept_half + from_partner(sent_half.astype(jnp.bfloat16), "ctx", bit_index).astype(
            sent_half.dtype
        )
    kv_grads = shaped.reshape(2, tokens, width_kv).astype(jnp.bfloat16)
    return (attn_rows, query_grad_rows, kv_grads[0], kv_grads[1])


def solution(mesh):
    in_specs = (
        P(("ctx", "head"), None),
        P(("ctx", "head"), None),
        P(("ctx", "head"), None),
        P(("ctx", "head"), None),
        P(),
        P(),
    )
    out_specs = (P("ctx", "head"), P("ctx", "head"), P("ctx", "head"), P("ctx", "head"))
    return jax.shard_map(body, mesh=mesh, in_specs=in_specs, out_specs=out_specs, check_vma=False)
```

profile of v0, /device:TPU:0, one launch (start us, length us, event | category | flops | bytes accessed | tf_op | source)
XLA Modules:
  0.0 1352.4 jit_solution(15705874742138274111)
XLA Ops:
  32.5 31.0 %all-to-all-done.5 = bf16[192,2,4096]{2,0,1:T(8,128)(2,1)S(1)} async-done(((bf16[192,2,4096]{2,0,1:T(8,128)(2,1)}), bf16[192,2,4096]{2,0,1:T(8,128)(2,1)S(1)}, u32[]{:S(2)}, u32[]{:S(2)}) %all-to-all-start.5) | async-done | bytes 3145760 | tf_op jit(solution)/shard_map/all_to_all | solution.py:203
  75.7 27.5 %all-to-all-done = bf16[192,2,4096]{2,0,1:T(8,128)(2,1)S(1)} async-done(((bf16[192,2,4096]{2,0,1:T(8,128)(2,1)}), bf16[192,2,4096]{2,0,1:T(8,128)(2,1)S(1)}, u32[]{:S(2)}, u32[]{:S(2)}) %all-to-all-start) | async-done | bytes 3145760 | tf_op jit(solution)/shard_map/all_to_all | solution.py:200
  113.3 72.8 %all-to-all-done.6 = bf16[3,128,4096]{2,0,1:T(4,128)(2,1)} async-done(((bf16[3,128,4096]{2,0,1:T(4,128)(2,1)}), bf16[3,128,4096]{2,0,1:T(4,128)(2,1)}, u32[]{:S(2)}, u32[]{:S(2)}) %all-to-all-start.6) | async-done | bytes 3145760 | tf_op jit(solution)/shard_map/all_to_all | solution.py:74
  186.1 19.7 %all-to-all-start.1 = ((bf16[3,128,4096]{2,0,1:T(4,128)(2,1)}), bf16[3,128,4096]{2,0,1:T(4,128)(2,1)}, u32[]{:S(2)}, u32[]{:S(2)}) async-start(bf16[3,128,4096]{2,0,1:T(4,128)(2,1)} %copy.126), calls=%async_computation.1 | async-start | bytes 8388608 | tf_op jit(solution)/shard_map/all_to_all | solution.py:67
  213.1 70.2 %all-to-all-done.1 = bf16[3,128,4096]{2,0,1:T(4,128)(2,1)} async-done(((bf16[3,128,4096]{2,0,1:T(4,128)(2,1)}), bf16[3,128,4096]{2,0,1:T(4,128)(2,1)}, u32[]{:S(2)}, u32[]{:S(2)}) %all-to-all-start.1) | async-done | bytes 3145760 | tf_op jit(solution)/shard_map/all_to_all | solution.py:67
  283.3 19.6 %all-to-all-start.7 = ((bf16[48,8,4096]{2,1,0:T(8,128)(2,1)}), bf16[48,8,4096]{2,1,0:T(8,128)(2,1)S(1)}, u32[]{:S(2)}, u32[]{:S(2)}) async-start(bf16[48,8,4096]{2,1,0:T(8,128)(2,1)} %gather_fusion.2), calls=%async_computation.7 | async-start | bytes 6291456 | tf_op jit(solution)/shard_map/all_to_all | solution.py:84
  318.1 44.2 %all-to-all-done.7 = bf16[48,8,4096]{2,1,0:T(8,128)(2,1)S(1)} async-done(((bf16[48,8,4096]{2,1,0:T(8,128)(2,1)}), bf16[48,8,4096]{2,1,0:T(8,128)(2,1)S(1)}, u32[]{:S(2)}, u32[]{:S(2)}) %all-to-all-start.7) | async-done | bytes 3145760 | tf_op jit(solution)/shard_map/all_to_all | solution.py:84
  362.3 15.5 %all-to-all-start.2 = ((bf16[48,8,4096]{2,1,0:T(8,128)(2,1)}), bf16[48,8,4096]{2,1,0:T(8,128)(2,1)}, u32[]{:S(2)}, u32[]{:S(2)}) async-start(bf16[48,8,4096]{2,1,0:T(8,128)(2,1)} %gather_fusion.1), calls=%async_computation.2 | async-start | bytes 6291456 | tf_op jit(solution)/shard_map/all_to_all | solution.py:83
  385.1 63.2 %collective-permute-done.1 = bf16[2,1,1,2,384,512]{5,4,3,0,2,1:T(8,128)(2,1)} collective-permute-done((bf16[2,1,1,2,384,512]{5,4,3,0,2,1:T(8,128)(2,1)}, bf16[2,1,1,2,384,512]{5,4,3,0,2,1:T(8,128)(2,1)}, u32[]{:S(2)}, u32[]{:S(2)}) %collective-permute-start.1) | collective-permute-done | bytes 1572896 | tf_op jit(solution)/shard_map/ppermute | solution.py:23
  488.8 688.4 %while.118 = (s32[]{:T(128)}, f32[2,24,128,512]{2,3,1,0:T(8,128)}, bf16[3,128,4,8,128]{4,3,2,1,0:T(8,128)(2,1)}, bf16[3,128,4,8,128]{4,3,2,1,0:T(8,128)(2,1)}, s...) while((s32[]{:T(128)}, f32[2,24,128,512]{2,3,1,0:T(8,128)}, ...), condition=%wide.region_13.14_spmd, body=%wide.region_3.13_spmd.sunk | while | flops 817209408 | bytes 121654488 | solution.py:240
  496.2 11.3 broadcast.251
  507.5 75.5 %while.119 = (s32[]{:T(128)}, f32[128,4,8]{0,2,1:T(8,128)S(1)}, f32[128,4,8]{0,2,1:T(8,128)S(1)}, f32[16,128,4,8,128]{1,4,3,2,0:T(8,128)}, s32[]{:T(128)}, /*ind...) while((s32[]{:T(128)}, f32[128,4,8]{0,2,1:T(8,128)S(1)}, ...), condition=%wide.region_7.7_spmd, body=%wide.region_4.6_spmd.sunk | while | flops 136880160 | bytes 10076686 | solution.py:130
  584.6 160.6 %while.120 = (s32[]{:T(128)}, f32[128,4,8,128]{0,3,2,1:T(8,128)}, s32[]{:T(128)}, s32[]{:T(128)}, s32[]{:T(128)}, /*index=5*/bf16[8,2,384,512]{2,3,1,0:T(8,128)(...) while((s32[]{:T(128)}, f32[128,4,8,128]{0,3,2,1:T(8,128)}, ...), condition=%wide.region_9.9_spmd, body=%wide.region_8.8_spmd.sunk | while | flops 135790624 | bytes 15090188 | solution.py:150
  754.7 187.3 %while.121 = (s32[]{:T(128)}, f32[128,4,8,128]{0,3,2,1:T(8,128)}, f32[2,24,128,512]{2,3,1,0:T(8,128)}, s32[]{:T(128)}, s32[]{:T(128)}, /*index=5*/s32[]{:T(128)}...) while((s32[]{:T(128)}, f32[128,4,8,128]{0,3,2,1:T(8,128)}, ...), condition=%wide.region_12.12_spmd, body=%wide.region_11.11_spmd.sunk | while | flops 540868608 | bytes 17744524 | solution.py:185
  955.0 11.3 broadcast.251
  966.3 14.1 %while.119 = (s32[]{:T(128)}, f32[128,4,8]{0,2,1:T(8,128)S(1)}, f32[128,4,8]{0,2,1:T(8,128)S(1)}, f32[16,128,4,8,128]{1,4,3,2,0:T(8,128)}, s32[]{:T(128)}, /*ind...) while((s32[]{:T(128)}, f32[128,4,8]{0,2,1:T(8,128)S(1)}, ...), condition=%wide.region_7.7_spmd, body=%wide.region_4.6_spmd.sunk | while | flops 136880160 | bytes 10076686 | solution.py:130
  982.0 30.1 %while.120 = (s32[]{:T(128)}, f32[128,4,8,128]{0,3,2,1:T(8,128)}, s32[]{:T(128)}, s32[]{:T(128)}, s32[]{:T(128)}, /*index=5*/bf16[8,2,384,512]{2,3,1,0:T(8,128)(...) while((s32[]{:T(128)}, f32[128,4,8,128]{0,3,2,1:T(8,128)}, ...), condition=%wide.region_9.9_spmd, body=%wide.region_8.8_spmd.sunk | while | flops 135790624 | bytes 15090188 | solution.py:150
  1021.7 35.1 %while.121 = (s32[]{:T(128)}, f32[128,4,8,128]{0,3,2,1:T(8,128)}, f32[2,24,128,512]{2,3,1,0:T(8,128)}, s32[]{:T(128)}, s32[]{:T(128)}, /*index=5*/s32[]{:T(128)}...) while((s32[]{:T(128)}, f32[128,4,8,128]{0,3,2,1:T(8,128)}, ...), condition=%wide.region_12.12_spmd, body=%wide.region_11.11_spmd.sunk | while | flops 540868608 | bytes 17744524 | solution.py:185
  1081.1 14.1 %while.119 = (s32[]{:T(128)}, f32[128,4,8]{0,2,1:T(8,128)S(1)}, f32[128,4,8]{0,2,1:T(8,128)S(1)}, f32[16,128,4,8,128]{1,4,3,2,0:T(8,128)}, s32[]{:T(128)}, /*ind...) while((s32[]{:T(128)}, f32[128,4,8]{0,2,1:T(8,128)S(1)}, ...), condition=%wide.region_7.7_spmd, body=%wide.region_4.6_spmd.sunk | while | flops 136880160 | bytes 10076686 | solution.py:130
  1096.8 30.1 %while.120 = (s32[]{:T(128)}, f32[128,4,8,128]{0,3,2,1:T(8,128)}, s32[]{:T(128)}, s32[]{:T(128)}, s32[]{:T(128)}, /*index=5*/bf16[8,2,384,512]{2,3,1,0:T(8,128)(...) while((s32[]{:T(128)}, f32[128,4,8,128]{0,3,2,1:T(8,128)}, ...), condition=%wide.region_9.9_spmd, body=%wide.region_8.8_spmd.sunk | while | flops 135790624 | bytes 15090188 | solution.py:150
  1136.5 35.1 %while.121 = (s32[]{:T(128)}, f32[128,4,8,128]{0,3,2,1:T(8,128)}, f32[2,24,128,512]{2,3,1,0:T(8,128)}, s32[]{:T(128)}, s32[]{:T(128)}, /*index=5*/s32[]{:T(128)}...) while((s32[]{:T(128)}, f32[128,4,8,128]{0,3,2,1:T(8,128)}, ...), condition=%wide.region_12.12_spmd, body=%wide.region_11.11_spmd.sunk | while | flops 540868608 | bytes 17744524 | solution.py:185
  1177.2 11.8 gather_fusion.3
  1217.0 70.2 %collective-permute-done.3 = bf16[2,1,2,2,3,128,512]{6,5,4,3,2,1,0:T(8,128)(2,1)S(1)} collective-permute-done((bf16[2,1,2,2,3,128,512]{6,5,4,3,2,1,0:T(8,128)(2,1)S(1)}, bf16[2,1,2,2,3,128,512]{6,5,4,3,2,1,0:T(8,128)(2,1)S(1)}, u32[]{:S(2)}, u32[]{:S(2)}) %collective-permute-start.3) | collective-permute-done | bytes 3145760 | tf_op jit(solution)/shard_map/ppermute | solution.py:23
  1297.7 35.7 %collective-permute-done.4 = bf16[2,1,1,2,3,128,512]{6,5,4,3,2,1,0:T(8,128)(2,1)S(1)} collective-permute-done((bf16[2,1,1,2,3,128,512]{6,5,4,3,2,1,0:T(8,128)(2,1)S(1)}, bf16[2,1,1,2,3,128,512]{6,5,4,3,2,1,0:T(8,128)(2,1)S(1)}, u32[]{:S(2)}, u32[]{:S(2)}) %collective-permute-start.4) | collective-permute-done | bytes 1572896 | tf_op jit(solution)/shard_map/ppermute | solution.py:23
  (633 shorter events, 775.4 us)
Async XLA Ops:
  0.6 17.6 %copy-start.5 = (bf16[192,8192]{1,0:T(8,128)(2,1)S(1)}, bf16[192,8192]{1,0:T(8,128)(2,1)}, u32[]{:S(2)}) copy-start(bf16[192,8192]{1,0:T(8,128)(2,1)} %param.17) | copy-start | bytes 9437188
  2.6 11.5 all-to-all-start.3
  14.1 10.5 all-to-all-start.4
  24.6 38.9 %all-to-all-start.5 = ((bf16[192,2,4096]{2,0,1:T(8,128)(2,1)}), bf16[192,2,4096]{2,0,1:T(8,128)(2,1)S(1)}, u32[]{:S(2)}, u32[]{:S(2)}) async-start(bf16[192,2,4096]{2,0,1:T(8,128)(2,1)} %bitcast.245), calls=%async_computation.5 | async-start | bytes 6291456 | tf_op jit(solution)/shard_map/all_to_all | solution.py:203
  65.2 38.0 %all-to-all-start = ((bf16[192,2,4096]{2,0,1:T(8,128)(2,1)}), bf16[192,2,4096]{2,0,1:T(8,128)(2,1)S(1)}, u32[]{:S(2)}, u32[]{:S(2)}) async-start(bf16[192,2,4096]{2,0,1:T(8,128)(2,1)} %bitcast.244), calls=%async_computation | async-start | bytes 6291456 | tf_op jit(solution)/shard_map/all_to_all | solution.py:200
  103.1 83.0 %all-to-all-start.6 = ((bf16[3,128,4096]{2,0,1:T(4,128)(2,1)}), bf16[3,128,4096]{2,0,1:T(4,128)(2,1)}, u32[]{:S(2)}, u32[]{:S(2)}) async-start(bf16[3,128,4096]{2,0,1:T(4,128)(2,1)} %copy.134), calls=%async_computation.6 | async-start | bytes 8388608 | tf_op jit(solution)/shard_map/all_to_all | solution.py:74
  113.3 92.5 %copy-start.7 = (s32[48]{0:T(128)S(1)}, s32[48]{0:T(128)}, u32[]{:S(2)}) copy-start(s32[48]{0:T(128)} %param.19) | copy-start | bytes 580
  186.1 97.2 %all-to-all-start.1 = ((bf16[3,128,4096]{2,0,1:T(4,128)(2,1)}), bf16[3,128,4096]{2,0,1:T(4,128)(2,1)}, u32[]{:S(2)}, u32[]{:S(2)}) async-start(bf16[3,128,4096]{2,0,1:T(4,128)(2,1)} %copy.126), calls=%async_computation.1 | async-start | bytes 8388608 | tf_op jit(solution)/shard_map/all_to_all | solution.py:67
  283.3 78.9 %all-to-all-start.7 = ((bf16[48,8,4096]{2,1,0:T(8,128)(2,1)}), bf16[48,8,4096]{2,1,0:T(8,128)(2,1)S(1)}, u32[]{:S(2)}, u32[]{:S(2)}) async-start(bf16[48,8,4096]{2,1,0:T(8,128)(2,1)} %gather_fusion.2), calls=%async_computation.7 | async-start | bytes 6291456 | tf_op jit(solution)/shard_map/all_to_all | solution.py:84
  305.3 72.5 %collective-permute-start = (bf16[1,1,1,2,384,512]{5,4,3,0,2,1:T(8,128)(2,1)}, bf16[1,1,1,2,384,512]{5,4,3,0,2,1:T(8,128)(2,1)}, u32[]{:S(2)}, u32[]{:S(2)}) collective-permute-start(bf16[1,1,1,2,384,512]{5,4,3,0,2,1:T(8,128)(2,1)} %get-tuple-element.1259), channel_id=1, source_target_pairs={{0,8},{2,10},{4,12},{6,14},{8,0},{10,2},{12,4},{14,6},{16,24},{18,... | collective-permute-start | bytes 2359304 | tf_op jit(solution)/shard_map/ppermute | solution.py:23
  362.3 115.8 %all-to-all-start.2 = ((bf16[48,8,4096]{2,1,0:T(8,128)(2,1)}), bf16[48,8,4096]{2,1,0:T(8,128)(2,1)}, u32[]{:S(2)}, u32[]{:S(2)}) async-start(bf16[48,8,4096]{2,1,0:T(8,128)(2,1)} %gather_fusion.1), calls=%async_computation.2 | async-start | bytes 6291456 | tf_op jit(solution)/shard_map/all_to_all | solution.py:83
  381.0 67.3 %collective-permute-start.1 = (bf16[2,1,1,2,384,512]{5,4,3,0,2,1:T(8,128)(2,1)}, bf16[2,1,1,2,384,512]{5,4,3,0,2,1:T(8,128)(2,1)}, u32[]{:S(2)}, u32[]{:S(2)}) collective-permute-start(bf16[2,1,1,2,384,512]{5,4,3,0,2,1:T(8,128)(2,1)} %maximum_select_fusion.2), channel_id=1, source_target_pairs={{0,4},{2,6},{4,0},{6,2},{8,12},{10,14},{12,8},{14,10},{16,20},{18,... | collective-permute-start | bytes 4718600 | tf_op jit(solution)/shard_map/ppermute | solution.py:23
  385.1 67.7 %copy-start.6 = (s32[2,3]{1,0:T(2,128)S(1)}, s32[2,3]{1,0:T(2,128)}, u32[]{:S(2)}) copy-start(s32[2,3]{1,0:T(2,128)} %param.18) | copy-start | bytes 76
  452.0 6.0 collective-permute-start.2
  745.2 4.3 copy-start
  766.4 3.9 copy-start.2
  1012.2 4.3 copy-start
  1126.9 4.3 copy-start
  1159.8 3.9 copy-start.2
  1206.1 81.2 %slice-start = ((s8[6291456]{0:T(1024)(128)(4,1)}), s8[2097152]{0:T(1024)(128)(4,1)S(1)}, s32[]{:S(2)}) async-start(s8[6291456]{0:T(1024)(128)(4,1)} %bitcast.234), calls=%async_computation.8 | async-start | bytes 4194304
  1212.8 74.5 %slice-start.1 = ((s8[6291456]{0:T(1024)(128)(4,1)}), s8[4194304]{0:T(1024)(128)(4,1)S(1)}, s32[]{:S(2)}) async-start(s8[6291456]{0:T(1024)(128)(4,1)} %bitcast.234), calls=%async_computation.9 | async-start | bytes 8388608
  1216.9 70.3 %collective-permute-start.3 = (bf16[2,1,2,2,3,128,512]{6,5,4,3,2,1,0:T(8,128)(2,1)S(1)}, bf16[2,1,2,2,3,128,512]{6,5,4,3,2,1,0:T(8,128)(2,1)S(1)}, u32[]{:S(2)}, u32[]{:S(2)}) collective-permute-start(bf16[2,1,2,2,3,128,512]{6,5,4,3,2,1,0:T(8,128)(2,1)S(1)} %select_convert_fusion), channel_id=1, source_target_pairs={{0,8},{2,10},{4,12},{6,14},{8,0},{10,2},{12,4},{14,6},{16,24},{18,... | collective-permute-start | bytes 9437192 | tf_op jit(solution)/shard_map/ppermute | solution.py:23
  1297.6 35.8 %collective-permute-start.4 = (bf16[2,1,1,2,3,128,512]{6,5,4,3,2,1,0:T(8,128)(2,1)S(1)}, bf16[2,1,1,2,3,128,512]{6,5,4,3,2,1,0:T(8,128)(2,1)S(1)}, u32[]{:S(2)}, u32[]{:S(2)}) collective-permute-start(bf16[2,1,1,2,3,128,512]{6,5,4,3,2,1,0:T(8,128)(2,1)S(1)} %select_convert_fusion.1), channel_id=1, source_target_pairs={{0,4},{2,6},{4,0},{6,2},{8,12},{10,14},{12,8},{14,10},{16,20},{18,... | collective-permute-start | bytes 4718600 | tf_op jit(solution)/shard_map/ppermute | solution.py:23
  1338.3 11.6 collective-permute-start.5
  (46 other events, 162.8 us)
where the time goes:
time: 1360 us; the launch traced here: 1350 us
  waiting for transfers between devices  428 us (31%)
  local copies, waits for them, and re-layouts  408 us (30%)
  matrix products  262 us (19%)
  other arithmetic  101 us (7%)
  starting transfers between devices  80.4 us (6%)
  loops' own time  72.1 us (5%)
    ppermute x6, waiting for transfers between devices, from_partner(): return lax.ppermute(value, axis, pairs)  172 us
    dynamic_slice x44, local copies, waits for them, and re-layouts, mix_values(): lax.dynamic_index_in_dim(logit_store, step_index, 0, keepdims=False)  111 us
    dot_general x22, matrix products, backprop(): jnp.einsum('tgrk,kgd->tgrd', dlogits, key_block, preferred_element_type=j...  74.4 us
    dot_general x22, matrix products, mix_values(): jnp.einsum('tgrk,kgd->tgrd', weights_low, value_block, preferred_element_...  74 us
    all_to_all x1, waiting for transfers between devices, move_blocks(): lax.all_to_all(second_rows.reshape(per_device, MASK_BLOCK_SIZE, row_width...  72.8 us
    all_to_all x1, waiting for transfers between devices, move_blocks(): lax.all_to_all(first_rows.reshape(per_device, MASK_BLOCK_SIZE, row_width)...  70.2 us
    dot_general x22, matrix products, backprop(): jnp.einsum('tgrd,kgd->tgrk', grad_block, value_block, preferred_element_t...  48 us
    dot_general x22, matrix products, backprop(): jnp.einsum('tgrk,tgrd->kgd', weights_low, grad_block, preferred_element_t...  45.1 us
  transfers between devices with their start and end apart: 14, of which 11 were waited for; matrix products, arithmetic and copies ran while one was open for 6% of the time, Pallas kernels for 0%

commit v1 on v0

v1 whole, which is shorter than its diff:
```python
from functools import partial
import math

import jax
import jax.numpy as jnp
from jax import lax
from jax.experimental import pallas as pl
from jax.experimental.pallas import tpu as pltpu
from jax.sharding import PartitionSpec as P

QUERY_HEADS = 64
KEY_VALUE_HEADS = 8
HEAD_SIZE = 128
MASK_BLOCK_SIZE = 128
GROUP_DEV = 8
GROUP_BLOCKS = 24
MOST = 16

RATIO = QUERY_HEADS // KEY_VALUE_HEADS
MASKED_LOGIT = -1e30
CHUNK = 256
SPAN_TOKENS = GROUP_BLOCKS * MASK_BLOCK_SIZE
MESH = pl.DeviceIdType.MESH


def doc_first(doc_blocks):
    ends = jnp.cumsum(doc_blocks)
    firsts = ends - doc_blocks
    blocks = jnp.arange(GROUP_BLOCKS, dtype=jnp.int32)
    return jnp.max(jnp.where(firsts[None, :] <= blocks[:, None], firsts[None, :], 0), axis=1)


def enter(peers):
    barrier = pltpu.get_barrier_semaphore()
    for peer in peers:
        pl.semaphore_signal(barrier, inc=1, device_id=peer, device_id_type=MESH)
    pl.semaphore_wait(barrier, len(peers))


def spread_kernel(
    head_dim, query_ref, grad_ref, key_ref, value_ref, *rest
):
    outs = rest[:4]
    stages = rest[4:8]
    send_sems, recv_sems, local_sems = rest[8:]
    sources = (query_ref, grad_ref, key_ref, value_ref)
    members = GROUP_DEV * head_dim
    rows = query_ref.shape[0]
    wide = outs[0].shape[1]
    heads = wide // HEAD_SIZE
    ctx = lax.axis_index("ctx")
    head = lax.axis_index("head")
    base = ctx // GROUP_DEV * GROUP_DEV
    lane = ctx - base
    own = lane * head_dim + head

    def place(step):
        peer = lax.rem(own + step, members)
        return peer // head_dim, lax.rem(peer, head_dim)

    def columns(peer_lane, peer_head):
        worker = peer_head * GROUP_DEV + peer_lane
        query_at = pl.ds(pl.multiple_of(worker * wide, HEAD_SIZE), wide)
        key_at = pl.ds(
            pl.multiple_of(worker * heads // RATIO * HEAD_SIZE, HEAD_SIZE), HEAD_SIZE
        )
        return (query_at, query_at, key_at, key_at)

    landing = pl.ds(pl.multiple_of(own * rows, 16), rows)
    own_columns = columns(lane, head)
    loads = []
    for index in range(4):
        load = pltpu.make_async_copy(
            sources[index].at[:, own_columns[index]], stages[index], local_sems.at[index]
        )
        load.start()
        loads.append(load)
    peers = [place(step) for step in range(1, members)]
    enter([{"ctx": base + peer_lane, "head": peer_head} for peer_lane, peer_head in peers])
    copies = []
    for step, (peer_lane, peer_head) in enumerate(peers):
        spots = columns(peer_lane, peer_head)
        for index in range(4):
            copy = pltpu.make_async_remote_copy(
                src_ref=sources[index].at[:, spots[index]],
                dst_ref=outs[index].at[landing, :],
                send_sem=send_sems.at[index, step],
                recv_sem=recv_sems.at[index, step],
                device_id={"ctx": base + peer_lane, "head": peer_head},
                device_id_type=MESH,
            )
            copy.start()
            copies.append(copy)
    stores = []
    for index in range(4):
        loads[index].wait()
        store = pltpu.make_async_copy(
            stages[index], outs[index].at[landing, :], local_sems.at[4 + index]
        )
        store.start()
        stores.append(store)
    for store in stores:
        store.wait()
    for copy in copies:
        copy.wait()


def spread(head_dim, query, grad, key, value):
    rows, width = query.shape
    members = GROUP_DEV * head_dim
    wide = width // members
    any_spec = pl.BlockSpec(memory_space=pl.ANY)
    return pl.pallas_call(
        partial(spread_kernel, head_dim),
        out_shape=[
            jax.ShapeDtypeStruct((rows * members, wide), jnp.bfloat16),
            jax.ShapeDtypeStruct((rows * members, wide), jnp.bfloat16),
            jax.ShapeDtypeStruct((rows * members, HEAD_SIZE), jnp.bfloat16),
            jax.ShapeDtypeStruct((rows * members, HEAD_SIZE), jnp.bfloat16),
        ],
        in_specs=[any_spec] * 4,
        out_specs=[any_spec] * 4,
        scratch_shapes=[
            pltpu.VMEM((rows, wide), jnp.bfloat16),
            pltpu.VMEM((rows, wide), jnp.bfloat16),
            pltpu.VMEM((rows, HEAD_SIZE), jnp.bfloat16),
            pltpu.VMEM((rows, HEAD_SIZE), jnp.bfloat16),
            pltpu.SemaphoreType.DMA((4, members - 1)),
            pltpu.SemaphoreType.DMA((4, members - 1)),
            pltpu.SemaphoreType.DMA((8,)),
        ],
        compiler_params=pltpu.CompilerParams(collective_id=0, has_side_effects=True),
        name="spread",
    )(query, grad, key, value)


def gather_kernel(attn_ref, query_ref, key_ref, value_ref, *rest):
    outs = rest[:4]
    stages = rest[4:8]
    send_sems, recv_sems, local_sems = rest[8:]
    sources = (attn_ref, query_ref, key_ref, value_ref)
    rows = outs[0].shape[0]
    wide = attn_ref.shape[1]
    ctx = lax.axis_index("ctx")
    head = lax.axis_index("head")
    base = ctx // GROUP_DEV * GROUP_DEV
    lane = ctx - base
    own_at = pl.ds(pl.multiple_of(lane * wide, HEAD_SIZE), wide)
    own_key_at = pl.ds(pl.multiple_of(lane * HEAD_SIZE, HEAD_SIZE), HEAD_SIZE)
    landing = (own_at, own_at, own_key_at, own_key_at)

    def taken(peer):
        return pl.ds(pl.multiple_of(peer * rows, 16), rows)

    loads = []
    for index in range(4):
        load = pltpu.make_async_copy(
            sources[index].at[taken(lane), :], stages[index], local_sems.at[index]
        )
        load.start()
        loads.append(load)
    peers = [lax.rem(lane + step, GROUP_DEV) for step in range(1, GROUP_DEV)]
    enter([{"ctx": base + peer, "head": head} for peer in peers])
    copies = []
    for step, peer in enumerate(peers):
        for index in range(4):
            copy = pltpu.make_async_remote_copy(
                src_ref=sources[index].at[taken(peer), :],
                dst_ref=outs[index].at[:, landing[index]],
                send_sem=send_sems.at[index, step],
                recv_sem=recv_sems.at[index, step],
                device_id={"ctx": base + peer, "head": head},
                device_id_type=MESH,
            )
            copy.start()
            copies.append(copy)
    stores = []
    for index in range(4):
        loads[index].wait()
        store = pltpu.make_async_copy(
            stages[index], outs[index].at[:, landing[index]], local_sems.at[4 + index]
        )
        store.start()
        stores.append(store)
    for store in stores:
        store.wait()
    for copy in copies:
        copy.wait()


def gather(attn, query, key, value):
    rows = attn.shape[0] // GROUP_DEV
    wide = attn.shape[1]
    any_spec = pl.BlockSpec(memory_space=pl.ANY)
    return pl.pallas_call(
        gather_kernel,
        out_shape=[
            jax.ShapeDtypeStruct((rows, wide * GROUP_DEV), jnp.bfloat16),
            jax.ShapeDtypeStruct((rows, wide * GROUP_DEV), jnp.bfloat16),
            jax.ShapeDtypeStruct((rows, HEAD_SIZE * GROUP_DEV), jnp.bfloat16),
            jax.ShapeDtypeStruct((rows, HEAD_SIZE * GROUP_DEV), jnp.bfloat16),
        ],
        in_specs=[any_spec] * 4,
        out_specs=[any_spec] * 4,
        scratch_shapes=[
            pltpu.VMEM((rows, wide), jnp.bfloat16),
            pltpu.VMEM((rows, wide), jnp.bfloat16),
            pltpu.VMEM((rows, HEAD_SIZE), jnp.bfloat16),
            pltpu.VMEM((rows, HEAD_SIZE), jnp.bfloat16),
            pltpu.SemaphoreType.DMA((4, GROUP_DEV - 1)),
            pltpu.SemaphoreType.DMA((4, GROUP_DEV - 1)),
            pltpu.SemaphoreType.DMA((8,)),
        ],
        compiler_params=pltpu.CompilerParams(collective_id=1, has_side_effects=True),
        name="gather",
    )(attn, query, key, value)


def dot(left, right):
    return jnp.dot(left, right, preferred_element_type=jnp.float32)


def attend_kernel(
    firsts_ref,
    places_ref,
    query_ref,
    grad_ref,
    key_ref,
    value_ref,
    attn_ref,
    query_grad_ref,
    key_grad_ref,
    value_grad_ref,
    keys,
    values,
    keys_t,
    values_t,
    store,
    out_t,
    query_grad_t,
    key_total,
    value_total,
):
    heads = query_ref.shape[1] // HEAD_SIZE
    block = MASK_BLOCK_SIZE
    columns = heads * block
    half = SPAN_TOKENS // 2
    scale = HEAD_SIZE ** (-0.5)
    scale_log2 = scale * math.log2(math.e)
    tail = keys.shape[0] - SPAN_TOKENS
    for source, flat, turned in ((key_ref, keys, keys_t), (value_ref, values, values_t)):
        flat[0:half, :] = source[half:SPAN_TOKENS, :]
        flat[half:SPAN_TOKENS, :] = source[0:half, :]
        flat[SPAN_TOKENS:, :] = jnp.zeros((tail, HEAD_SIZE), jnp.bfloat16)
        turned[:, SPAN_TOKENS:] = jnp.zeros((HEAD_SIZE, tail), jnp.bfloat16)
    for index in range(GROUP_BLOCKS):
        at = slice(index * block, (index + 1) * block)
        keys_t[:, at] = keys[at, :].T
        values_t[:, at] = values[at, :].T
    key_total[...] = jnp.zeros_like(key_total)
    value_total[...] = jnp.zeros_like(value_total)
    token = lax.rem(lax.broadcasted_iota(jnp.int32, (CHUNK, columns), 1), block)
    key_at = lax.broadcasted_iota(jnp.int32, (CHUNK, columns), 0)
    ahead = key_at - token

    def one_block(index, _):
        first = firsts_ref[index]
        count = index - first + 1
        steps = (count * block + CHUNK - 1) // CHUNK
        loader = lax.rem(index + GROUP_BLOCKS // 2, GROUP_BLOCKS)
        source = pl.ds(pl.multiple_of(loader * block, block), block)
        target = pl.ds(pl.multiple_of(places_ref[loader] * block, block), block)
        parts = [slice(h * HEAD_SIZE, (h + 1) * HEAD_SIZE) for h in range(heads)]
        query = jnp.concatenate([query_ref[source, at] for at in parts], axis=0)
        grad = jnp.concatenate([grad_ref[source, at] for at in parts], axis=0)
        query_t = jnp.concatenate([query_ref[source, at].T for at in parts], axis=1)
        grad_t = jnp.concatenate([grad_ref[source, at].T for at in parts], axis=1)

        def spot(step):
            return pl.ds(pl.multiple_of(first * block + step * CHUNK, block), CHUNK)

        def slot(step):
            return pl.ds(pl.multiple_of(step * CHUNK, CHUNK), CHUNK)

        def logits(step, peak):
            raw = dot(keys[spot(step), :], query_t)
            bound = (count - 1) * block - step * CHUNK
            raw = jnp.where(ahead <= bound, raw, MASKED_LOGIT)
            store[slot(step), :] = raw
            return jnp.maximum(peak, jnp.max(raw, axis=0, keepdims=True))

        peak = lax.fori_loop(
            0, steps, logits, jnp.full((1, columns), MASKED_LOGIT, jnp.float32)
        )
        peak = peak * scale_log2
        out_t[...] = jnp.zeros_like(out_t)

        def mix(step, total):
            mass = jnp.exp2(store[slot(step), :] * scale_log2 - peak)
            store[slot(step), :] = mass
            out_t[...] += dot(values_t[:, spot(step)], mass.astype(jnp.bfloat16))
            return total + jnp.sum(mass, axis=0, keepdims=True)

        total = lax.fori_loop(0, steps, mix, jnp.zeros((1, columns), jnp.float32))
        share = 1.0 / total
        out = (out_t[...] * share).astype(jnp.bfloat16)
        delta = jnp.sum(
            out.astype(jnp.float32) * grad_t.astype(jnp.float32), axis=0, keepdims=True
        )
        for h, at in enumerate(parts):
            attn_ref[target, at] = out[:, h * block : (h + 1) * block].T
        query_grad_t[...] = jnp.zeros_like(query_grad_t)

        def back(step, carry):
            weights = store[slot(step), :] * share
            value_total[spot(step), :] += dot(weights.astype(jnp.bfloat16), grad)
            grad_weights = dot(values[spot(step), :], grad_t)
            dlogits = (weights * (grad_weights - delta)).astype(jnp.bfloat16)
            key_total[spot(step), :] += dot(dlogits, query)
            query_grad_t[...] += dot(keys_t[:, spot(step)], dlogits)
            return carry

        lax.fori_loop(0, steps, back, 0)
        moved = (query_grad_t[...] * scale).astype(jnp.bfloat16)
        for h, at in enumerate(parts):
            query_grad_ref[target, at] = moved[:, h * block : (h + 1) * block].T
        return 0

    lax.fori_loop(0, GROUP_BLOCKS, one_block, 0)

    def finish(index, _):
        loader = lax.rem(index + GROUP_BLOCKS // 2, GROUP_BLOCKS)
        source = pl.ds(pl.multiple_of(index * block, block), block)
        target = pl.ds(pl.multiple_of(places_ref[loader] * block, block), block)
        key_grad_ref[target, :] = (key_total[source, :] * scale).astype(jnp.bfloat16)
        value_grad_ref[target, :] = value_total[source, :].astype(jnp.bfloat16)
        return 0

    lax.fori_loop(0, GROUP_BLOCKS, finish, 0)


def attend(firsts, places, query, grad, key, value):
    wide = query.shape[1]
    columns = wide // HEAD_SIZE * MASK_BLOCK_SIZE
    padded = SPAN_TOKENS + CHUNK - MASK_BLOCK_SIZE
    vmem = pl.BlockSpec(memory_space=pltpu.VMEM)
    smem = pl.BlockSpec(memory_space=pltpu.SMEM)
    return pl.pallas_call(
        attend_kernel,
        out_shape=[
            jax.ShapeDtypeStruct(query.shape, jnp.bfloat16),
            jax.ShapeDtypeStruct(query.shape, jnp.bfloat16),
            jax.ShapeDtypeStruct(key.shape, jnp.bfloat16),
            jax.ShapeDtypeStruct(key.shape, jnp.bfloat16),
        ],
        in_specs=[smem, smem, vmem, vmem, vmem, vmem],
        out_specs=[vmem] * 4,
        scratch_shapes=[
            pltpu.VMEM((padded, HEAD_SIZE), jnp.bfloat16),
            pltpu.VMEM((padded, HEAD_SIZE), jnp.bfloat16),
            pltpu.VMEM((HEAD_SIZE, padded), jnp.bfloat16),
            pltpu.VMEM((HEAD_SIZE, padded), jnp.bfloat16),
            pltpu.VMEM((MOST * MASK_BLOCK_SIZE, columns), jnp.float32),
            pltpu.VMEM((HEAD_SIZE, columns), jnp.float32),
            pltpu.VMEM((HEAD_SIZE, columns), jnp.float32),
            pltpu.VMEM((padded, HEAD_SIZE), jnp.float32),
            pltpu.VMEM((padded, HEAD_SIZE), jnp.float32),
        ],
        compiler_params=pltpu.CompilerParams(vmem_limit_bytes=60 * 1024 * 1024),
        name="attend",
    )(firsts, places, query, grad, key, value)


def body(head_dim, query_rows, key_rows, value_rows, grad_rows, doc_blocks, block_perm):
    group = lax.axis_index("ctx") // GROUP_DEV
    firsts = doc_first(lax.dynamic_index_in_dim(doc_blocks, group, 0, keepdims=False))
    places = lax.dynamic_slice_in_dim(block_perm, group * GROUP_BLOCKS, GROUP_BLOCKS)
    places = places - group * GROUP_BLOCKS
    query, grad, key, value = spread(head_dim, query_rows, grad_rows, key_rows, value_rows)
    results = attend(firsts, places, query, grad, key, value)
    attn, query_grad, key_parts, value_parts = gather(*results)
    heads = query.shape[1] // HEAD_SIZE
    sharers = max(RATIO // heads, 1)

    def joined(parts):
        rows = parts.shape[0]
        shaped = parts.reshape(rows, -1, sharers, HEAD_SIZE).astype(jnp.float32)
        return jnp.sum(shaped, axis=2).astype(jnp.bfloat16).reshape(rows, -1)

    return attn, query_grad, joined(key_parts), joined(value_parts)


def solution(mesh):
    split = P(("ctx", "head"), None)
    out_spec = P("ctx", "head")
    return jax.shard_map(
        partial(body, mesh.shape["head"]),
        mesh=mesh,
        in_specs=(split, split, split, split, P(), P()),
        out_specs=(out_spec,) * 4,
        check_vma=False,
    )
```

time: 1360 us -> 333 us (0.24)
  waiting for transfers between devices: 428 us -> 0 us
  local copies, waits for them, and re-layouts: 408 us -> 13.9 us
  Pallas kernels: 0 us -> 308 us
  matrix products: 262 us -> 0 us
  other arithmetic: 101 us -> 9.98 us
  starting transfers between devices: 80.4 us -> 0 us
  loops' own time: 72.1 us -> 0 us
    pallas_call x0 -> x3, Pallas kernels: none -> 308 us  [the longest x1 121 us: spread(): pl.pallas_call(partial(spread_kernel, head_dim), out_shape=[jax.ShapeDtyp...]
    dot_general x132 -> x0, matrix products: 262 us -> none  [the longest x22 74.4 us: backprop(): jnp.einsum('tgrk,kgd->tgrd', dlogits, key_block, preferred_element_type=j...]
    all_to_all x8 -> x0, waiting for transfers between devices: 256 us -> none  [the longest x1 72.8 us: move_blocks(): lax.all_to_all(second_rows.reshape(per_device, MASK_BLOCK_SIZE, row_width...]
    ppermute x6 -> x0, waiting for transfers between devices: 172 us -> none  [from_partner(): return lax.ppermute(value, axis, pairs)]
    dynamic_slice x62 -> x1, local copies, waits for them, and re-layouts: 138 us -> 0.68 us  [body(): lax.dynamic_index_in_dim(doc_blocks, group, 0, keepdims=False)]
    all_to_all x8 -> x0, starting transfers between devices: 76.5 us -> none  [the longest x1 19.7 us: move_blocks(): lax.all_to_all(first_rows.reshape(per_device, MASK_BLOCK_SIZE, row_width)...]
    slice x68 -> x0, local copies, waits for them, and re-layouts: 73.9 us -> none  [the longest x44 42.2 us: kv_block(): kv_piece[0, 1].reshape(MASK_BLOCK_SIZE, kv_heads, HEAD_SIZE)]
    another operation x10 -> x0, loops' own time: 72.1 us -> none  [the longest x3 30.6 us: attend_block(): lax.fori_loop(0, key_count, softmax_stats, (jnp.full(row_shape, MASKED_LO...]
  transfers between devices with their start and end apart: 14 -> 0, of which waited for: 11 -> 0; matrix products, arithmetic and copies ran while one was open for 6% -> 0% of each run, Pallas kernels for 0% -> 0%
where the time goes in v1:
time: 333 us; the launch traced here: 332 us
  Pallas kernels  308 us (92%)
  local copies, waits for them, and re-layouts  13.9 us (4%)
  other arithmetic  9.98 us (3%)
    pallas_call x1, Pallas kernels, spread(): pl.pallas_call(partial(spread_kernel, head_dim), out_shape=[jax.ShapeDtyp...  121 us
    pallas_call x1, Pallas kernels, attend(): pl.pallas_call(attend_kernel, out_shape=[jax.ShapeDtypeStruct(query.shape...  96.3 us
    pallas_call x1, Pallas kernels, gather(): pl.pallas_call(gather_kernel, out_shape=[jax.ShapeDtypeStruct((rows, wide...  90.1 us
    reduce_sum x2, other arithmetic, joined(): return jnp.sum(shaped, axis=2).astype(jnp.bfloat16).reshape(rows, -1)  7.28 us

profile of v1, /device:TPU:0, one launch (start us, length us, event | category | flops | bytes accessed | tf_op | source)
XLA Modules:
  0.0 332.4 jit_solution(11053173193917243702)
XLA Ops:
  0.7 1.2 dynamic-slice_subtract_fusion.places_ref
  1.9 0.7 constant_dynamic-slice_fusion
  2.6 0.2 reduce-window_clone.1
  2.8 0.7 subtract_bitcast_fusion
  3.4 0.6 select_reduce_fusion.firsts_ref
  4.0 121.4 %spread.1 = (bf16[3072,512]{1,0:T(8,128)(2,1)}, bf16[3072,512]{1,0:T(8,128)(2,1)}, bf16[3072,128]{1,0:T(8,128)(2,1)}, bf16[3072,128]{1,0:T(8,128)(2,1)}) custom-call(bf16[192,8192]{1,0:T(8,128)(2,1)} %query_ref.1, bf16[192,8192]{1,0:T(8,128)(2,1)} %grad_ref.1, bf16[192,1024]{1,0:T(8,128)(2,1)} %key_ref.1, bf16[192,1024]{1,0:T(8,128)(2,1)} %value_ref.1), custom_call_target="tpu_custom_call" | custom-call | tf_op jit(solution)/shard_map/spread/pallas_call | solution.py:113
  125.5 96.3 %attend.1 = (bf16[3072,512]{1,0:T(8,128)(2,1)}, bf16[3072,512]{1,0:T(8,128)(2,1)}, bf16[3072,128]{1,0:T(8,128)(2,1)}, bf16[3072,128]{1,0:T(8,128)(2,1)}) custom-call(s32[24]{0:T(128)} %select_reduce_fusion.firsts_ref, s32[24]{0:T(128)} %dynamic-slice_subtract_fusion.places_ref, bf16[3072,512]{1,0:T(8,128)(2,1)} %get-tuple-element.16.query_ref, ...), custom_call_target="tpu_custom_call" | custom-call | tf_op jit(solution)/shard_map/attend/pallas_call | solution.py:348
  221.8 90.1 %gather.1 = (bf16[384,4096]{1,0:T(8,128)(2,1)}, bf16[384,4096]{1,0:T(8,128)(2,1)}, bf16[384,1024]{1,0:T(8,128)(2,1)}, bf16[384,1024]{1,0:T(8,128)(2,1)}) custom-call(bf16[3072,512]{1,0:T(8,128)(2,1)} %get-tuple-element.20.attn_ref, bf16[3072,512]{1,0:T(8,128)(2,1)} %get-tuple-element.21.query_ref, bf16[3072,128]{1,0:T(8,128)(2,1)} %get-tuple-element.22.key_ref, ...), custom_call_target="tpu_custom_call" | custom-call | tf_op jit(solution)/shard_map/gather/pallas_call | solution.py:195
  312.0 3.3 reshape.26
  315.2 0.0 copy-start.1
  315.2 3.3 %reduce_sum.24 = bf16[384,4,128]{2,1,0:T(4,128)(2,1)S(1)} reduce(bf16[384,4,2,128]{3,2,1,0:T(2,128)(2,1)} %reshape.26, bf16[]{:T(256)} %constant.40.clone.1), dimensions={2}, to_apply=%region_2.3 | reduce | flops 196608 | bytes 1179650 | tf_op jit(solution)/shard_map/reduce_sum | solution.py:388
  318.6 3.3 reshape.28
  321.8 3.9 %reduce_sum.25 = bf16[384,4,128]{2,1,0:T(4,128)(2,1)} reduce(bf16[384,4,2,128]{3,2,1,0:T(2,128)(2,1)} %reshape.28, bf16[]{:T(256)} %constant.40.clone.1), dimensions={2}, to_apply=%region_3.4 | reduce | flops 196608 | bytes 1179650 | tf_op jit(solution)/shard_map/reduce_sum | solution.py:388
  325.8 2.0 copy_bitcast_fusion
  327.7 0.0 copy-done.1
  327.7 0.0 copy-start
  327.7 1.7 copy.16
  329.4 1.4 copy-done
  330.8 1.7 copy.17
Async XLA Ops:
  315.2 12.5 %copy-start.1 = (bf16[384,4096]{1,0:T(8,128)(2,1)S(1)}, bf16[384,4096]{1,0:T(8,128)(2,1)}, u32[]{:S(2)}) copy-start(bf16[384,4096]{1,0:T(8,128)(2,1)} %get-tuple-element.34) | copy-start | bytes 9437188
  327.7 3.0 copy-start

commit v2 on v1

--- a/solution.py
+++ b/solution.py
@@ -37,26 +37,35 @@
     pl.semaphore_wait(barrier, len(peers))
 
 
-def spread_kernel(
-    head_dim, query_ref, grad_ref, key_ref, value_ref, *rest
-):
-    outs = rest[:4]
-    stages = rest[4:8]
-    send_sems, recv_sems, local_sems = rest[8:]
-    sources = (query_ref, grad_ref, key_ref, value_ref)
+def flipped(index, mask, count):
+    result, bit = index, 1
+    while bit < count:
+        if mask & bit:
+            result = result + bit - index // bit % 2 * (2 * bit)
+        bit *= 2
+    return result
+
+
+def visiting_order(members):
+    return SPREAD_ORDER if len(SPREAD_ORDER) == members - 1 else list(range(members - 1, 0, -1))
+
+
+SPREAD_ORDER = [13, 5, 9, 15, 7, 11, 12, 4, 8, 14, 6, 10, 1, 3, 2]
+
+
+def spread_kernel(head_dim, query_ref, grad_ref, pair_ref, *rest):
+    query_out, grad_out, pair_out, query_stage, grad_stage, pair_stage = rest[:6]
+    send_sems, recv_sems, pass_send_sems, pass_recv_sems, local_sems = rest[6:]
     members = GROUP_DEV * head_dim
     rows = query_ref.shape[0]
-    wide = outs[0].shape[1]
+    wide = query_out.shape[1]
     heads = wide // HEAD_SIZE
     ctx = lax.axis_index("ctx")
     head = lax.axis_index("head")
     base = ctx // GROUP_DEV * GROUP_DEV
     lane = ctx - base
     own = lane * head_dim + head
-
-    def place(step):
-        peer = lax.rem(own + step, members)
-        return peer // head_dim, lax.rem(peer, head_dim)
+    order = visiting_order(members)
 
     def columns(peer_lane, peer_head):
         worker = peer_head * GROUP_DEV + peer_lane
@@ -64,48 +73,97 @@
         key_at = pl.ds(
             pl.multiple_of(worker * heads // RATIO * HEAD_SIZE, HEAD_SIZE), HEAD_SIZE
         )
-        return (query_at, query_at, key_at, key_at)
-
-    landing = pl.ds(pl.multiple_of(own * rows, 16), rows)
-    own_columns = columns(lane, head)
-    loads = []
-    for index in range(4):
-        load = pltpu.make_async_copy(
-            sources[index].at[:, own_columns[index]], stages[index], local_sems.at[index]
-        )
+        return query_at, key_at
+
+    def rows_of(member):
+        return pl.ds(pl.multiple_of(member * rows, 16), rows)
+
+    landing = rows_of(own)
+    kind = lane % 2
+    query_at, key_at = columns(lane, head)
+    loads = [
+        pltpu.make_async_copy(pair_ref.at[kind, :, key_at], pair_stage, local_sems.at[0]),
+        pltpu.make_async_copy(query_ref.at[:, query_at], query_stage, local_sems.at[1]),
+        pltpu.make_async_copy(grad_ref.at[:, query_at], grad_stage, local_sems.at[2]),
+    ]
+    for load in loads:
         load.start()
-        loads.append(load)
-    peers = [place(step) for step in range(1, members)]
-    enter([{"ctx": base + peer_lane, "head": peer_head} for peer_lane, peer_head in peers])
-    copies = []
-    for step, (peer_lane, peer_head) in enumerate(peers):
-        spots = columns(peer_lane, peer_head)
-        for index in range(4):
+    peers = []
+    for mask in order:
+        member = flipped(own, mask, members)
+        peers.append((member, member // head_dim, member % head_dim))
+    device = [{"ctx": base + peer_lane, "head": peer_head} for _, peer_lane, peer_head in peers]
+    sibling = {"ctx": base + flipped(lane, 1, GROUP_DEV), "head": head}
+    enter(device)
+    pair_copies, copies = [], []
+    for step, (member, peer_lane, peer_head) in enumerate(peers):
+        key_at = columns(peer_lane, peer_head)[1]
+        copy = pltpu.make_async_remote_copy(
+            src_ref=pair_ref.at[peer_lane % 2, :, key_at],
+            dst_ref=pair_out.at[peer_lane % 2, landing, :],
+            send_sem=send_sems.at[2, step],
+            recv_sem=recv_sems.at[2, step],
+            device_id=device[step],
+            device_id_type=MESH,
+        )
+        copy.start()
+        pair_copies.append(copy)
+    for step, (member, peer_lane, peer_head) in enumerate(peers):
+        query_at = columns(peer_lane, peer_head)[0]
+        for index, (source, target) in enumerate(
+            ((query_ref, query_out), (grad_ref, grad_out))
+        ):
             copy = pltpu.make_async_remote_copy(
-                src_ref=sources[index].at[:, spots[index]],
-                dst_ref=outs[index].at[landing, :],
+                src_ref=source.at[:, query_at],
+                dst_ref=target.at[landing, :],
                 send_sem=send_sems.at[index, step],
                 recv_sem=recv_sems.at[index, step],
-                device_id={"ctx": base + peer_lane, "head": peer_head},
+                device_id=device[step],
                 device_id_type=MESH,
             )
             copy.start()
             copies.append(copy)
     stores = []
-    for index in range(4):
+    for index, (stage, target) in enumerate(
+        (
+            (pair_stage, pair_out.at[kind, landing, :]),
+            (query_stage, query_out.at[landing, :]),
+            (grad_stage, grad_out.at[landing, :]),
+        )
+    ):
         loads[index].wait()
-        store = pltpu.make_async_copy(
-            stages[index], outs[index].at[landing, :], local_sems.at[4 + index]
-        )
+        store = pltpu.make_async_copy(stage, target, local_sems.at[3 + index])
         store.start()
         stores.append(store)
+
+    def passing(slot, source, spot):
+        copy = pltpu.make_async_remote_copy(
+            src_ref=source,
+            dst_ref=pair_out.at[kind, spot, :],
+            send_sem=pass_send_sems.at[slot],
+            recv_sem=pass_recv_sems.at[slot],
+            device_id=sibling,
+            device_id_type=MESH,
+        )
+        copy.start()
+        return copy
+
+    passes = [passing(members - 1, pair_stage, landing)]
+    for step, (member, peer_lane, peer_head) in enumerate(peers):
+        pair_copies[step].wait_recv()
+        spot = rows_of(member)
+        passes.append(passing(step, pair_out.at[kind, spot, :], spot))
     for store in stores:
         store.wait()
+    for copy in pair_copies:
+        copy.wait_send()
     for copy in copies:
         copy.wait()
-
-
-def spread(head_dim, query, grad, key, value):
+    for copy in passes:
+        copy.wait()
+
+
+def spread(head_dim, query, grad, pair):
     rows, width = query.shape
     members = GROUP_DEV * head_dim
     wide = width // members
@@ -115,105 +173,139 @@
         out_shape=[
             jax.ShapeDtypeStruct((rows * members, wide), jnp.bfloat16),
             jax.ShapeDtypeStruct((rows * members, wide), jnp.bfloat16),
-            jax.ShapeDtypeStruct((rows * members, HEAD_SIZE), jnp.bfloat16),
-            jax.ShapeDtypeStruct((rows * members, HEAD_SIZE), jnp.bfloat16),
-        ],
-        in_specs=[any_spec] * 4,
-        out_specs=[any_spec] * 4,
+            jax.ShapeDtypeStruct((2, rows * members, HEAD_SIZE), jnp.bfloat16),
+        ],
+        in_specs=[any_spec] * 3,
+        out_specs=[any_spec] * 3,
         scratch_shapes=[
             pltpu.VMEM((rows, wide), jnp.bfloat16),
             pltpu.VMEM((rows, wide), jnp.bfloat16),
             pltpu.VMEM((rows, HEAD_SIZE), jnp.bfloat16),
-            pltpu.VMEM((rows, HEAD_SIZE), jnp.bfloat16),
-            pltpu.SemaphoreType.DMA((4, members - 1)),
-            pltpu.SemaphoreType.DMA((4, members - 1)),
-            pltpu.SemaphoreType.DMA((8,)),
+            pltpu.SemaphoreType.DMA((3, members - 1)),
+            pltpu.SemaphoreType.DMA((3, members - 1)),
+            pltpu.SemaphoreType.DMA((members,)),
+            pltpu.SemaphoreType.DMA((members,)),
+            pltpu.SemaphoreType.DMA((6,)),
         ],
         compiler_params=pltpu.CompilerParams(collective_id=0, has_side_effects=True),
         name="spread",
-    )(query, grad, key, value)
-
-
-def gather_kernel(attn_ref, query_ref, key_ref, value_ref, *rest):
-    outs = rest[:4]
-    stages = rest[4:8]
-    send_sems, recv_sems, local_sems = rest[8:]
-    sources = (attn_ref, query_ref, key_ref, value_ref)
-    rows = outs[0].shape[0]
+    )(query, grad, pair)
+
+
+def gather_kernel(attn_ref, query_ref, pair_ref, *rest):
+    attn_out, query_out, pair_out, attn_stage, query_stage, mine, other = rest[:7]
+    send_sems, recv_sems, swap_sems, local_sems = rest[7:]
+    rows = attn_out.shape[0]
     wide = attn_ref.shape[1]
+    sharers = RATIO // (wide // HEAD_SIZE)
     ctx = lax.axis_index("ctx")
     head = lax.axis_index("head")
     base = ctx // GROUP_DEV * GROUP_DEV
     lane = ctx - base
+    kind = lane % 2
     own_at = pl.ds(pl.multiple_of(lane * wide, HEAD_SIZE), wide)
-    own_key_at = pl.ds(pl.multiple_of(lane * HEAD_SIZE, HEAD_SIZE), HEAD_SIZE)
-    landing = (own_at, own_at, own_key_at, own_key_at)
+    pair_at = pl.ds(pl.multiple_of(lane // sharers * HEAD_SIZE, HEAD_SIZE), HEAD_SIZE)
+    pair_landing = pair_out.at[kind, lane % sharers // 2, :, pair_at]
 
     def taken(peer):
         return pl.ds(pl.multiple_of(peer * rows, 16), rows)
 
-    loads = []
-    for index in range(4):
-        load = pltpu.make_async_copy(
-            sources[index].at[taken(lane), :], stages[index], local_sems.at[index]
-        )
+    loads = [
+        pltpu.make_async_copy(pair_ref.at[kind], mine, local_sems.at[0]),
+        pltpu.make_async_copy(attn_ref.at[taken(lane), :], attn_stage, local_sems.at[1]),
+        pltpu.make_async_copy(query_ref.at[taken(lane), :], query_stage, local_sems.at[2]),
+    ]
+    for load in loads:
         load.start()
-        loads.append(load)
-    peers = [lax.rem(lane + step, GROUP_DEV) for step in range(1, GROUP_DEV)]
-    enter([{"ctx": base + peer, "head": head} for peer in peers])
+    peers = [flipped(lane, mask, GROUP_DEV) for mask in GATHER_ORDER]
+    device = [{"ctx": base + peer, "head": head} for peer in peers]
+    enter(device)
+    swap = pltpu.make_async_remote_copy(
+        src_ref=pair_ref.at[1 - kind],
+        dst_ref=other,
+        send_sem=swap_sems.at[0],
+        recv_sem=swap_sems.at[1],
+        device_id={"ctx": base + flipped(lane, 1, GROUP_DEV), "head": head},
+        device_id_type=MESH,
+    )
+    swap.start()
     copies = []
     for step, peer in enumerate(peers):
-        for index in range(4):
+        for index, (source, target) in enumerate(((attn_ref, attn_out), (query_ref, query_out))):
             copy = pltpu.make_async_remote_copy(
-                src_ref=sources[index].at[taken(peer), :],
-                dst_ref=outs[index].at[:, landing[index]],
+                src_ref=source.at[taken(peer), :],
+                dst_ref=target.at[:, own_at],
                 send_sem=send_sems.at[index, step],
                 recv_sem=recv_sems.at[index, step],
-                device_id={"ctx": base + peer, "head": head},
+                device_id=device[step],
                 device_id_type=MESH,
             )
             copy.start()
             copies.append(copy)
     stores = []
-    for index in range(4):
+    for index, (stage, target) in ((1, (attn_stage, attn_out)), (2, (query_stage, query_out))):
         loads[index].wait()
-        store = pltpu.make_async_copy(
-            stages[index], outs[index].at[:, landing[index]], local_sems.at[4 + index]
-        )
+        store = pltpu.make_async_copy(stage, target.at[:, own_at], local_sems.at[2 + index])
         store.start()
         stores.append(store)
+    loads[0].wait()
+    swap.wait()
+    for peer in range(GROUP_DEV):
+        at = slice(peer * rows, (peer + 1) * rows)
+        total = mine[at, :].astype(jnp.float32) + other[at, :].astype(jnp.float32)
+        mine[at, :] = total.astype(jnp.bfloat16)
+    store = pltpu.make_async_copy(mine.at[taken(lane), :], pair_landing, local_sems.at[5])
+    store.start()
+    stores.append(store)
+    for step, peer in enumerate(peers):
+        copy = pltpu.make_async_remote_copy(
+            src_ref=mine.at[taken(peer), :],
+            dst_ref=pair_landing,
+            send_sem=send_sems.at[2, step],
+            recv_sem=recv_sems.at[2, step],
+            device_id=device[step],
+            device_id_type=MESH,
+        )
+        copy.start()
+        copies.append(copy)
     for store in stores:
         store.wait()
     for copy in copies:
         copy.wait()
 
 
-def gather(attn, query, key, value):
-    rows = attn.shape[0] // GROUP_DEV
-    wide = attn.shape[1]
+GATHER_ORDER = [6, 2, 4, 7, 3, 5, 1]
+
+
+def gather(attn, query, pair):
+    tokens, wide = attn.shape
+    rows = tokens // GROUP_DEV
+    sharers = RATIO // (wide // HEAD_SIZE)
     any_spec = pl.BlockSpec(memory_space=pl.ANY)
     return pl.pallas_call(
         gather_kernel,
         out_shape=[
             jax.ShapeDtypeStruct((rows, wide * GROUP_DEV), jnp.bfloat16),
             jax.ShapeDtypeStruct((rows, wide * GROUP_DEV), jnp.bfloat16),
-            jax.ShapeDtypeStruct((rows, HEAD_SIZE * GROUP_DEV), jnp.bfloat16),
-            jax.ShapeDtypeStruct((rows, HEAD_SIZE * GROUP_DEV), jnp.bfloat16),
-        ],
-        in_specs=[any_spec] * 4,
-        out_specs=[any_spec] * 4,
+            jax.ShapeDtypeStruct(
+                (2, sharers // 2, rows, HEAD_SIZE * GROUP_DEV // sharers), jnp.bfloat16
+            ),
+        ],
+        in_specs=[any_spec] * 3,
+        out_specs=[any_spec] * 3,
         scratch_shapes=[
             pltpu.VMEM((rows, wide), jnp.bfloat16),
             pltpu.VMEM((rows, wide), jnp.bfloat16),
-            pltpu.VMEM((rows, HEAD_SIZE), jnp.bfloat16),
-            pltpu.VMEM((rows, HEAD_SIZE), jnp.bfloat16),
-            pltpu.SemaphoreType.DMA((4, GROUP_DEV - 1)),
-            pltpu.SemaphoreType.DMA((4, GROUP_DEV - 1)),
-            pltpu.SemaphoreType.DMA((8,)),
+            pltpu.VMEM((tokens, HEAD_SIZE), jnp.bfloat16),
+            pltpu.VMEM((tokens, HEAD_SIZE), jnp.bfloat16),
+            pltpu.SemaphoreType.DMA((3, GROUP_DEV - 1)),
+            pltpu.SemaphoreType.DMA((3, GROUP_DEV - 1)),
+            pltpu.SemaphoreType.DMA((2,)),
+            pltpu.SemaphoreType.DMA((6,)),
         ],
         compiler_params=pltpu.CompilerParams(collective_id=1, has_side_effects=True),
         name="gather",
-    )(attn, query, key, value)
+    )(attn, query, pair)
 
 
 def dot(left, right):
@@ -225,12 +317,10 @@
     places_ref,
     query_ref,
     grad_ref,
-    key_ref,
-    value_ref,
+    pair_ref,
     attn_ref,
     query_grad_ref,
-    key_grad_ref,
-    value_grad_ref,
+    pair_grad_ref,
     keys,
     values,
     keys_t,
@@ -248,9 +338,9 @@
     scale = HEAD_SIZE ** (-0.5)
     scale_log2 = scale * math.log2(math.e)
     tail = keys.shape[0] - SPAN_TOKENS
-    for source, flat, turned in ((key_ref, keys, keys_t), (value_ref, values, values_t)):
-        flat[0:half, :] = source[half:SPAN_TOKENS, :]
-        flat[half:SPAN_TOKENS, :] = source[0:half, :]
+    for kind, flat, turned in ((0, keys, keys_t), (1, values, values_t)):
+        flat[0:half, :] = pair_ref[kind, half:SPAN_TOKENS, :]
+        flat[half:SPAN_TOKENS, :] = pair_ref[kind, 0:half, :]
         flat[SPAN_TOKENS:, :] = jnp.zeros((tail, HEAD_SIZE), jnp.bfloat16)
         turned[:, SPAN_TOKENS:] = jnp.zeros((HEAD_SIZE, tail), jnp.bfloat16)
     for index in range(GROUP_BLOCKS):
@@ -332,14 +422,14 @@
         loader = lax.rem(index + GROUP_BLOCKS // 2, GROUP_BLOCKS)
         source = pl.ds(pl.multiple_of(index * block, block), block)
         target = pl.ds(pl.multiple_of(places_ref[loader] * block, block), block)
-        key_grad_ref[target, :] = (key_total[source, :] * scale).astype(jnp.bfloat16)
-        value_grad_ref[target, :] = value_total[source, :].astype(jnp.bfloat16)
+        pair_grad_ref[0, target, :] = (key_total[source, :] * scale).astype(jnp.bfloat16)
+        pair_grad_ref[1, target, :] = value_total[source, :].astype(jnp.bfloat16)
         return 0
 
     lax.fori_loop(0, GROUP_BLOCKS, finish, 0)
 
 
-def attend(firsts, places, query, grad, key, value):
+def attend(firsts, places, query, grad, pair):
     wide = query.shape[1]
     columns = wide // HEAD_SIZE * MASK_BLOCK_SIZE
     padded = SPAN_TOKENS + CHUNK - MASK_BLOCK_SIZE
@@ -350,11 +440,10 @@
         out_shape=[
             jax.ShapeDtypeStruct(query.shape, jnp.bfloat16),
             jax.ShapeDtypeStruct(query.shape, jnp.bfloat16),
-            jax.ShapeDtypeStruct(key.shape, jnp.bfloat16),
-            jax.ShapeDtypeStruct(key.shape, jnp.bfloat16),
-        ],
-        in_specs=[smem, smem, vmem, vmem, vmem, vmem],
-        out_specs=[vmem] * 4,
+            jax.ShapeDtypeStruct(pair.shape, jnp.bfloat16),
+        ],
+        in_specs=[smem, smem, vmem, vmem, vmem],
+        out_specs=[vmem] * 3,
         scratch_shapes=[
             pltpu.VMEM((padded, HEAD_SIZE), jnp.bfloat16),
             pltpu.VMEM((padded, HEAD_SIZE), jnp.bfloat16),
@@ -368,7 +457,7 @@
         ],
         compiler_params=pltpu.CompilerParams(vmem_limit_bytes=60 * 1024 * 1024),
         name="attend",
-    )(firsts, places, query, grad, key, value)
+    )(firsts, places, query, grad, pair)
 
 
 def body(head_dim, query_rows, key_rows, value_rows, grad_rows, doc_blocks, block_perm):
@@ -376,18 +465,13 @@
     firsts = doc_first(lax.dynamic_index_in_dim(doc_blocks, group, 0, keepdims=False))
     places = lax.dynamic_slice_in_dim(block_perm, group * GROUP_BLOCKS, GROUP_BLOCKS)
     places = places - group * GROUP_BLOCKS
-    query, grad, key, value = spread(head_dim, query_rows, grad_rows, key_rows, value_rows)
-    results = attend(firsts, places, query, grad, key, value)
-    attn, query_grad, key_parts, value_parts = gather(*results)
-    heads = query.shape[1] // HEAD_SIZE
-    sharers = max(RATIO // heads, 1)
-
-    def joined(parts):
-        rows = parts.shape[0]
-        shaped = parts.reshape(rows, -1, sharers, HEAD_SIZE).astype(jnp.float32)
-        return jnp.sum(shaped, axis=2).astype(jnp.bfloat16).reshape(rows, -1)
-
-    return attn, query_grad, joined(key_parts), joined(value_parts)
+    query, grad, pair = spread(head_dim, query_rows, grad_rows, jnp.stack([key_rows, value_rows]))
+    attn, query_grad, parts = gather(*attend(firsts, places, query, grad, pair))
+    if parts.shape[1] > 1:
+        parts = jnp.sum(parts.astype(jnp.float32), axis=1).astype(jnp.bfloat16)
+    else:
+        parts = parts[:, 0]
+    return attn, query_grad, parts[0], parts[1]
 
 
 def solution(mesh):

time: 333 us -> 281 us (0.84)
  Pallas kernels: 308 us -> 267 us
  local copies, waits for them, and re-layouts: 13.9 us -> 8.45 us
  other arithmetic: 9.98 us -> 4.77 us
    pallas_call x1, Pallas kernels: 121 us -> 92.4 us  [spread(): pl.pallas_call(partial(spread_kernel, head_dim), out_shape=[jax.ShapeDtyp...]
    pallas_call x1, Pallas kernels: 90.1 us -> 79.3 us  [gather(): pl.pallas_call(gather_kernel, out_shape=[jax.ShapeDtypeStruct((rows, wide...]
    reshape x3 -> x0, local copies, waits for them, and re-layouts: 8.49 us -> none  [the longest x2 6.51 us: joined(): shaped = parts.reshape(rows, -1, sharers, HEAD_SIZE).astype(jnp.float32)]
    reduce_sum x2 -> x0, other arithmetic: 7.28 us -> none  [joined(): return jnp.sum(shaped, axis=2).astype(jnp.bfloat16).reshape(rows, -1)]
where the time goes in v2:
time: 281 us
  Pallas kernels  267 us (95%)
  local copies, waits for them, and re-layouts  8.45 us (3%)
  other arithmetic  4.77 us (2%)
    pallas_call x1, Pallas kernels, attend(): pl.pallas_call(attend_kernel, out_shape=[jax.ShapeDtypeStruct(query.shape...  95.5 us
    pallas_call x1, Pallas kernels, spread(): pl.pallas_call(partial(spread_kernel, head_dim), out_shape=[jax.ShapeDtyp...  92.4 us
    pallas_call x1, Pallas kernels, gather(): pl.pallas_call(gather_kernel, out_shape=[jax.ShapeDtypeStruct((rows, wide...  79.3 us
    unnamed x4, local copies, waits for them, and re-layouts  5.72 us

profile of v2, /device:TPU:0, one launch (start us, length us, event | category | flops | bytes accessed | tf_op | source)
XLA Modules:
  0.0 281.1 jit_solution(16789926611141968532)
XLA Ops:
  0.7 1.2 dynamic-slice_subtract_fusion.places_ref
  1.9 0.7 constant_dynamic-slice_fusion
  2.6 0.2 reduce-window_clone.1
  2.8 0.7 subtract_bitcast_fusion
  3.4 0.6 select_reduce_fusion.firsts_ref
  4.0 2.1 pad_maximum_fusion.pair_ref
  6.1 92.4 %spread.1 = (bf16[3072,512]{1,0:T(8,128)(2,1)}, bf16[3072,512]{1,0:T(8,128)(2,1)}, bf16[2,3072,128]{2,1,0:T(8,128)(2,1)}) custom-call(bf16[192,8192]{1,0:T(8,128)(2,1)} %query_ref.1, bf16[192,8192]{1,0:T(8,128)(2,1)} %grad_ref.1, bf16[2,192,1024]{2,1,0:T(8,128)(2,1)} %pad_maximum_fusion.pair_ref), custom_call_target="tpu_custom_call" | custom-call | tf_op jit(solution)/shard_map/spread/pallas_call | solution.py:171
  98.5 95.5 %attend.1 = (bf16[3072,512]{1,0:T(8,128)(2,1)}, bf16[3072,512]{1,0:T(8,128)(2,1)}, bf16[2,3072,128]{2,1,0:T(8,128)(2,1)}) custom-call(s32[24]{0:T(128)} %select_reduce_fusion.firsts_ref, s32[24]{0:T(128)} %dynamic-slice_subtract_fusion.places_ref, bf16[3072,512]{1,0:T(8,128)(2,1)} %get-tuple-element.13.query_ref, ...), custom_call_target="tpu_custom_call" | custom-call | tf_op jit(solution)/shard_map/attend/pallas_call | solution.py:438
  194.0 79.3 %gather.1 = (bf16[384,4096]{1,0:T(8,128)(2,1)}, bf16[384,4096]{1,0:T(8,128)(2,1)}, bf16[2,1,384,512]{3,2,1,0:T(8,128)(2,1)}) custom-call(bf16[3072,512]{1,0:T(8,128)(2,1)} %get-tuple-element.16.attn_ref, bf16[3072,512]{1,0:T(8,128)(2,1)} %get-tuple-element.17.query_ref, bf16[2,3072,128]{2,1,0:T(8,128)(2,1)} %get-tuple-element.18.pair_ref), custom_call_target="tpu_custom_call" | custom-call | tf_op jit(solution)/shard_map/gather/pallas_call | solution.py:285
  273.3 2.0 slice_bitcast_fusion
  275.4 0.0 copy-start
  275.4 4.1 %copy.12 = bf16[384,4096]{1,0:T(8,128)(2,1)} copy(bf16[384,4096]{1,0:T(8,128)(2,1)} %get-tuple-element.28) | data formatting | bytes 6291456
  279.4 0.0 copy-done
  279.4 1.7 copy.13
Async XLA Ops:
  275.4 4.1 %copy-start = (bf16[384,4096]{1,0:T(8,128)(2,1)S(1)}, bf16[384,4096]{1,0:T(8,128)(2,1)}, u32[]{:S(2)}) copy-start(bf16[384,4096]{1,0:T(8,128)(2,1)} %get-tuple-element.29) | copy-start | bytes 9437188

commit v3 on v2

--- a/solution.py
+++ b/solution.py
@@ -18,7 +18,7 @@
 
 RATIO = QUERY_HEADS // KEY_VALUE_HEADS
 MASKED_LOGIT = -1e30
-CHUNK = 256
+CHUNK = 512
 SPAN_TOKENS = GROUP_BLOCKS * MASK_BLOCK_SIZE
 MESH = pl.DeviceIdType.MESH
 

time: 281 us -> 264 us (0.940)
  Pallas kernels: 267 us -> 249 us
    pallas_call x1, Pallas kernels: 95.5 us -> 77.7 us  [attend(): pl.pallas_call(attend_kernel, out_shape=[jax.ShapeDtypeStruct(query.shape...]
where the time goes in v3:
time: 264 us; the launch traced here: 263 us
  Pallas kernels  249 us (94%)
  local copies, waits for them, and re-layouts  8.45 us (3%)
  other arithmetic  4.77 us (2%)
    pallas_call x1, Pallas kernels, spread(): pl.pallas_call(partial(spread_kernel, head_dim), out_shape=[jax.ShapeDtyp...  92.4 us
    pallas_call x1, Pallas kernels, gather(): pl.pallas_call(gather_kernel, out_shape=[jax.ShapeDtypeStruct((rows, wide...  79.3 us
    pallas_call x1, Pallas kernels, attend(): pl.pallas_call(attend_kernel, out_shape=[jax.ShapeDtypeStruct(query.shape...  77.7 us
    unnamed x4, local copies, waits for them, and re-layouts  5.72 us

profile of v3, /device:TPU:0, one launch (start us, length us, event | category | flops | bytes accessed | tf_op | source)
XLA Modules:
  0.0 263.3 jit_solution(17049834914718690996)
XLA Ops:
  0.7 1.2 dynamic-slice_subtract_fusion.places_ref
  1.9 0.7 constant_dynamic-slice_fusion
  2.6 0.2 reduce-window_clone.1
  2.8 0.7 subtract_bitcast_fusion
  3.4 0.6 select_reduce_fusion.firsts_ref
  4.0 2.1 pad_maximum_fusion.pair_ref
  6.1 92.4 %spread.1 = (bf16[3072,512]{1,0:T(8,128)(2,1)}, bf16[3072,512]{1,0:T(8,128)(2,1)}, bf16[2,3072,128]{2,1,0:T(8,128)(2,1)}) custom-call(bf16[192,8192]{1,0:T(8,128)(2,1)} %query_ref.1, bf16[192,8192]{1,0:T(8,128)(2,1)} %grad_ref.1, bf16[2,192,1024]{2,1,0:T(8,128)(2,1)} %pad_maximum_fusion.pair_ref), custom_call_target="tpu_custom_call" | custom-call | tf_op jit(solution)/shard_map/spread/pallas_call | solution.py:171
  98.5 77.7 %attend.1 = (bf16[3072,512]{1,0:T(8,128)(2,1)}, bf16[3072,512]{1,0:T(8,128)(2,1)}, bf16[2,3072,128]{2,1,0:T(8,128)(2,1)}) custom-call(s32[24]{0:T(128)} %select_reduce_fusion.firsts_ref, s32[24]{0:T(128)} %dynamic-slice_subtract_fusion.places_ref, bf16[3072,512]{1,0:T(8,128)(2,1)} %get-tuple-element.13.query_ref, ...), custom_call_target="tpu_custom_call" | custom-call | tf_op jit(solution)/shard_map/attend/pallas_call | solution.py:438
  176.2 79.3 %gather.1 = (bf16[384,4096]{1,0:T(8,128)(2,1)}, bf16[384,4096]{1,0:T(8,128)(2,1)}, bf16[2,1,384,512]{3,2,1,0:T(8,128)(2,1)}) custom-call(bf16[3072,512]{1,0:T(8,128)(2,1)} %get-tuple-element.16.attn_ref, bf16[3072,512]{1,0:T(8,128)(2,1)} %get-tuple-element.17.query_ref, bf16[2,3072,128]{2,1,0:T(8,128)(2,1)} %get-tuple-element.18.pair_ref), custom_call_target="tpu_custom_call" | custom-call | tf_op jit(solution)/shard_map/gather/pallas_call | solution.py:285
  255.5 2.0 slice_bitcast_fusion
  257.6 0.0 copy-start
  257.6 4.1 %copy.12 = bf16[384,4096]{1,0:T(8,128)(2,1)} copy(bf16[384,4096]{1,0:T(8,128)(2,1)} %get-tuple-element.28) | data formatting | bytes 6291456
  261.6 0.0 copy-done
  261.6 1.7 copy.13
Async XLA Ops:
  257.6 4.1 %copy-start = (bf16[384,4096]{1,0:T(8,128)(2,1)S(1)}, bf16[384,4096]{1,0:T(8,128)(2,1)}, u32[]{:S(2)}) copy-start(bf16[384,4096]{1,0:T(8,128)(2,1)} %get-tuple-element.29) | copy-start | bytes 9437188
